TPU v7x, 32 devices: a whole 2x2x4 slice. The times are simulated.
32 devices in a mesh: dp: 8 (over y, x, core), tensor: 4 (over z).
Axes of the slice: x: 2, y: 2, z: 4, core: 2. Of those that a mesh axis runs over, the one named last changes fastest.
Arguments:
- tokens: bfloat16 [16384, 1024], P(('dp', 'tensor')), may hold values from -6 to 6
- cotangent: bfloat16 [16384, 1024], P(('dp', 'tensor')), may hold values from -6 to 6
- lengths: int32 [32], replicated, may hold values from 1 to 1024, as said below
- deal: int32 [32], replicated, may hold values from 0 to 31, as said below
- w_qkv: bfloat16 [3, 1024, 1024], P(None, 'dp', 'tensor'), may hold values from -0.1875 to 0.1875
- w_o: bfloat16 [1024, 1024], P('tensor', 'dp'), may hold values from -0.1875 to 0.1875
- w_1: bfloat16 [1024, 4096], P('dp', 'tensor'), may hold values from -0.1875 to 0.1875
- w_2: bfloat16 [4096, 1024], P('tensor', 'dp'), may hold values from -0.09375 to 0.09375
- b_qv: float32 [2, 1024], P(None, 'tensor'), may hold values from -1.8 to 1.8
- b_o: float32 [1024], replicated, may hold values from -0.3 to 0.3
- b_1: float32 [4096], P('tensor'), may hold values from -1.8 to 1.8
- b_2: float32 [1024], replicated, may hold values from -1.2 to 1.2
- ln_gain: float32 [4, 1024], replicated, may hold values from 0.25 to 1.75
- ln_bias: float32 [4, 1024], replicated, may hold values from -1.8 to 1.8
Outputs:
- output: bfloat16 [16384, 1024], P(('dp', 'tensor'))
- input_grad: bfloat16 [16384, 1024], P(('dp', 'tensor'))
- w_qkv_grad: float32 [3, 1024, 1024], P(None, 'dp', 'tensor')
- w_o_grad: float32 [1024, 1024], P('tensor', 'dp')
- w_1_grad: float32 [1024, 4096], P('dp', 'tensor')
- w_2_grad: float32 [4096, 1024], P('tensor', 'dp')
- b_qv_grad: float32 [2, 1024], P(None, 'tensor')
- b_o_grad: float32 [1024], replicated
- b_1_grad: float32 [4096], P('tensor')
- b_2_grad: float32 [1024], replicated
- ln_gain_grad: float32 [4, 1024], replicated
- ln_bias_grad: float32 [4, 1024], replicated
Inputs may be any that keep to these rules, and one draw needn't show every extreme that they name: The 4 sequences that deal gives to one data group have lengths that sum to 2048, and one of them has exactly 1024 tokens. `deal`: A permutation of the sequences; slots b * 4 to b * 4 + 3 belong to data group b.
All inputs are finite; a program needn't handle non-finite values. Where the computation divides by a largest or mean magnitude, that divisor is 1e-20 or more.
Results may differ from a plain program's by a relative error of at most 0.015.
Values may be sent and summed in bfloat16 or wider, within the bound.
A program may use at most 192 MiB of HBM per device.

v0:
```python
from functools import partial
import math
import jax
import jax.numpy as jnp
from jax import lax
from jax.sharding import PartitionSpec as P

DH = 64
MAXLEN = 1024
QBLK = 512
NORM_EPS = 1e-05
RELAX_FACTOR = 32.0
MASKED_OUT = -1000000000.0


def scaled_norm(values, norm_gain, norm_shift):
    peak = jnp.max(jnp.abs(values), axis=-1, keepdims=True) + NORM_EPS
    scaled = values / peak
    centred = scaled - jnp.mean(scaled, axis=-1, keepdims=True)
    spread = jnp.mean(centred * centred, axis=-1, keepdims=True)
    return centred * lax.rsqrt(spread + NORM_EPS) * norm_gain + norm_shift


def norm_back(values, norm_gain, norm_shift, row_grad):
    result, pull = jax.vjp(scaled_norm, values, norm_gain, norm_shift)
    return pull(row_grad)


def segment_of(seq_lens, row_total):
    seq_ends = jnp.cumsum(seq_lens)
    token_positions = jnp.arange(row_total, dtype=jnp.int32)
    return jnp.sum((token_positions[:, None] >= seq_ends[None, :]).astype(jnp.int32), axis=1)


def lane_gather(rows_low):
    return lax.all_gather(rows_low, "tensor", axis=0, tiled=True)


def lane_sum(term_fn, rows_here):
    return lax.psum_scatter(
        term_fn(jnp.int32(0), rows_here * lax.axis_size("tensor")).astype(jnp.bfloat16),
        "tensor",
        scatter_dimension=0,
        tiled=True,
    ).astype(jnp.float32)


def grad_gather(rows_low):
    return lax.all_gather(rows_low, "tensor", axis=0, tiled=True)


def grad_sum(term_fn, rows_here):
    return lax.psum_scatter(
        term_fn(jnp.int32(0), rows_here * lax.axis_size("tensor")).astype(jnp.bfloat16),
        "tensor",
        scatter_dimension=0,
        tiled=True,
    ).astype(jnp.float32)


def window_of(block_index, query_heads, key_pad, value_pad, segment, seg_pad):
    span = QBLK + MAXLEN
    first = block_index * QBLK
    query_block = lax.dynamic_slice_in_dim(query_heads, first, QBLK, 0)
    key_block = lax.dynamic_slice_in_dim(key_pad, first, span, 0)
    value_block = lax.dynamic_slice_in_dim(value_pad, first, span, 0)
    query_seg = lax.dynamic_slice_in_dim(segment, first, QBLK, 0)
    key_seg = lax.dynamic_slice_in_dim(seg_pad, first, span, 0)
    query_pos = first + jnp.arange(QBLK, dtype=jnp.int32)
    key_pos = first - MAXLEN + jnp.arange(span, dtype=jnp.int32)
    allowed = (key_pos[None, :] <= query_pos[:, None]) & (key_seg[None, :] == query_seg[:, None])
    return (query_block, key_block, value_block, allowed)


def block_scores(query_block, key_block, allowed):
    factor = 1.0 / (RELAX_FACTOR * math.sqrt(DH))
    raw_score = (
        jnp.einsum("qhd,khd->hqk", query_block, key_block, preferred_element_type=jnp.float32)
        * factor
    )
    return jnp.where(allowed[None], raw_score, MASKED_OUT)


def attn_forward(query_heads, key_pad, value_pad, segment, seg_pad):
    row_total = query_heads.shape[0]

    def one_block(block_index):
        query_block, key_block, value_block, allowed = window_of(
            block_index, query_heads, key_pad, value_pad, segment, seg_pad
        )
        masked = block_scores(query_block, key_block, allowed)
        row_peak = jnp.max(masked, axis=-1, keepdims=True)
        exponent = jnp.exp(RELAX_FACTOR * (masked - row_peak))
        row_totals = jnp.sum(exponent, axis=-1, keepdims=True)
        attn_prob = (exponent / row_totals).astype(jnp.bfloat16)
        mixed = jnp.einsum(
            "hqk,khd->qhd", attn_prob, value_block, preferred_element_type=jnp.float32
        )
        return (mixed.astype(jnp.bfloat16), row_peak, row_totals)

    mixed_all, peaks, sums_all = lax.map(one_block, jnp.arange(row_total // QBLK, dtype=jnp.int32))
    return (mixed_all.reshape(row_total, -1), peaks, sums_all)


def attn_backward(query_heads, key_pad, value_pad, segment, seg_pad, peaks, sums_all, grad_heads):
    row_total = query_heads.shape[0]
    span = QBLK + MAXLEN
    factor = 1.0 / (RELAX_FACTOR * math.sqrt(DH))
    start_grads = (jnp.zeros(key_pad.shape, jnp.float32), jnp.zeros(value_pad.shape, jnp.float32))

    def one_step(carry, block_index):
        key_grad, value_grad = carry
        first = block_index * QBLK
        query_block, key_block, value_block, allowed = window_of(
            block_index, query_heads, key_pad, value_pad, segment, seg_pad
        )
        grad_block = lax.dynamic_slice_in_dim(grad_heads, first, QBLK, 0)
        masked = block_scores(query_block, key_block, allowed)
        exponent = jnp.exp(RELAX_FACTOR * (masked - peaks[block_index]))
        attn_prob = exponent / sums_all[block_index]
        prob_low = attn_prob.astype(jnp.bfloat16)
        grad_prob = jnp.einsum(
            "qhd,khd->hqk", grad_block, value_block, preferred_element_type=jnp.float32
        )
        value_term = jnp.einsum(
            "hqk,qhd->khd", prob_low, grad_block, preferred_element_type=jnp.float32
        )
        inner = jnp.sum(grad_prob * attn_prob, axis=-1, keepdims=True)
        grad_score = jnp.where(
            allowed[None], RELAX_FACTOR * attn_prob * (grad_prob - inner), 0.0
        ).astype(jnp.bfloat16)
        query_term = (
            jnp.einsum("hqk,khd->qhd", grad_score, key_block, preferred_element_type=jnp.float32)
            * factor
        )
        key_term = (
            jnp.einsum("hqk,qhd->khd", grad_score, query_block, preferred_element_type=jnp.float32)
            * factor
        )
        key_grad = lax.dynamic_update_slice_in_dim(
            key_grad, lax.dynamic_slice_in_dim(key_grad, first, span, 0) + key_term, first, 0
        )
        value_grad = lax.dynamic_update_slice_in_dim(
            value_grad, lax.dynamic_slice_in_dim(value_grad, first, span, 0) + value_term, first, 0
        )
        return ((key_grad, value_grad), query_term)

    (key_grad, value_grad), query_terms = lax.scan(
        one_step, start_grads, jnp.arange(row_total // QBLK, dtype=jnp.int32)
    )
    query_grad = query_terms.reshape(row_total, -1)
    return (
        query_grad,
        key_grad[MAXLEN:].reshape(row_total, -1),
        value_grad[MAXLEN:].reshape(row_total, -1),
    )


def body(
    tokens, cotangent, lengths, deal, w_qkv, w_o, w_1, w_2, b_qv, b_o, b_1, b_2, ln_gain, ln_bias
):
    local_in, local_cot = (
        lax.all_to_all(tokens, "dp", split_axis=0, concat_axis=0, tiled=True),
        lax.all_to_all(cotangent, "dp", split_axis=0, concat_axis=0, tiled=True),
    )
    lane_count = lax.axis_size("tensor")
    group_index = lax.axis_index("dp")
    rows_here = local_in.shape[0]
    row_total = rows_here * lane_count
    seq_per = lengths.shape[0] // lax.axis_size("dp")
    picked = lax.dynamic_slice_in_dim(deal, group_index * seq_per, seq_per)
    lookup = picked[:, None] == jnp.arange(lengths.shape[0], dtype=jnp.int32)[None, :]
    seq_lens = jnp.sum(jnp.where(lookup, lengths[None, :], 0), axis=1)
    segment = segment_of(seq_lens, row_total)
    seg_pad = jnp.concatenate([jnp.full((MAXLEN,), -1, jnp.int32), segment])
    qkv_full, out_full = (
        lax.all_gather(w_qkv, "dp", axis=1, tiled=True),
        lax.all_gather(w_o, "dp", axis=1, tiled=True),
    )
    local_width = qkv_full.shape[2]
    head_count = local_width // DH
    hidden = local_in.astype(jnp.float32)
    normed_in = lane_gather(scaled_norm(hidden, ln_gain[0], ln_bias[0]).astype(jnp.bfloat16))
    projected = jnp.einsum("rd,sde->sre", normed_in, qkv_full, preferred_element_type=jnp.float32)
    query_rows = (projected[0] + b_qv[0]).astype(jnp.bfloat16)
    key_rows = projected[1].astype(jnp.bfloat16)
    value_rows = (projected[2] + b_qv[1]).astype(jnp.bfloat16)
    head_shape = (row_total, head_count, DH)
    pad_rows = jnp.zeros((MAXLEN, head_count, DH), jnp.bfloat16)
    query_heads = query_rows.reshape(head_shape)
    key_pad = jnp.concatenate([pad_rows, key_rows.reshape(head_shape)], 0)
    value_pad = jnp.concatenate([pad_rows, value_rows.reshape(head_shape)], 0)
    heads_out, peaks, sums_all = attn_forward(query_heads, key_pad, value_pad, segment, seg_pad)

    def out_term(first_row, row_count):
        return jnp.dot(heads_out, out_full, preferred_element_type=jnp.float32)

    attn_out = lane_sum(out_term, rows_here) + b_o
    first_sum = hidden + scaled_norm(attn_out, ln_gain[1], ln_bias[1])
    normed_mid = lane_gather(scaled_norm(first_sum, ln_gain[2], ln_bias[2]).astype(jnp.bfloat16))
    up_full, down_full = (
        lax.all_gather(w_1, "dp", axis=0, tiled=True),
        lax.all_gather(w_2, "dp", axis=1, tiled=True),
    )
    pre_act = jnp.dot(normed_mid, up_full, preferred_element_type=jnp.float32) + b_1
    act = jax.nn.gelu(pre_act, approximate=False).astype(jnp.bfloat16)

    def down_term(first_row, row_count):
        return jnp.dot(act, down_full, preferred_element_type=jnp.float32)

    feedforward_output = lane_sum(down_term, rows_here) + b_2
    result = first_sum + scaled_norm(feedforward_output, ln_gain[3], ln_bias[3])
    grad_result = local_cot.astype(jnp.float32)
    grad_ffn, gain_three, shift_three = norm_back(
        feedforward_output, ln_gain[3], ln_bias[3], grad_result
    )
    grad_ffn_low = grad_ffn.astype(jnp.bfloat16)
    bias_two_grad = jnp.sum(grad_ffn_low.astype(jnp.float32), axis=0)
    grad_ffn_full = grad_gather(grad_ffn_low)
    up_back, down_back = (
        lax.all_gather(w_1, "dp", axis=0, tiled=True),
        lax.all_gather(w_2, "dp", axis=1, tiled=True),
    )
    grad_act = jnp.einsum("rd,fd->rf", grad_ffn_full, down_back, preferred_element_type=jnp.float32)
    down_grad = jnp.einsum("rf,rd->fd", act, grad_ffn_full, preferred_element_type=jnp.float32)
    gelu_value, gelu_pull = jax.vjp(partial(jax.nn.gelu, approximate=False), pre_act)
    grad_pre = gelu_pull(grad_act)[0].astype(jnp.bfloat16)
    bias_one_grad = jnp.sum(grad_pre.astype(jnp.float32), axis=0)
    up_grad = jnp.einsum("rd,rf->df", normed_mid, grad_pre, preferred_element_type=jnp.float32)
    up_shard, down_shard = (up_grad, down_grad)

    def mid_term(first_row, row_count):
        return jnp.einsum("rf,df->rd", grad_pre, up_back, preferred_element_type=jnp.float32)

    grad_mid = grad_sum(mid_term, rows_here)
    grad_first_part, gain_two, shift_two = norm_back(first_sum, ln_gain[2], ln_bias[2], grad_mid)
    grad_first = grad_result + grad_first_part
    grad_attn, gain_one, shift_one = norm_back(attn_out, ln_gain[1], ln_bias[1], grad_first)
    grad_attn_low = grad_attn.astype(jnp.bfloat16)
    bias_out_grad = jnp.sum(grad_attn_low.astype(jnp.float32), axis=0)
    grad_attn_full = grad_gather(grad_attn_low)
    qkv_back, out_back = (
        lax.all_gather(w_qkv, "dp", axis=1, tiled=True),
        lax.all_gather(w_o, "dp", axis=1, tiled=True),
    )
    grad_heads = jnp.einsum(
        "rd,ed->re", grad_attn_full, out_back, preferred_element_type=jnp.float32
    ).astype(jnp.bfloat16)
    out_grad = jnp.einsum(
        "re,rd->ed", heads_out, grad_attn_full, preferred_element_type=jnp.float32
    )
    query_grad, key_grad, value_grad = attn_backward(
        query_heads,
        key_pad,
        value_pad,
        segment,
        seg_pad,
        peaks,
        sums_all,
        grad_heads.reshape(head_shape),
    )
    grad_qkv = jnp.stack([query_grad, key_grad, value_grad]).astype(jnp.bfloat16)
    grad_qkv_wide = grad_qkv.astype(jnp.float32)
    bias_qv_grad = jnp.stack([jnp.sum(grad_qkv_wide[0], axis=0), jnp.sum(grad_qkv_wide[2], axis=0)])
    qkv_grad = jnp.einsum("rd,sre->sde", normed_in, grad_qkv, preferred_element_type=jnp.float32)

    def input_term(first_row, row_count):
        return jnp.einsum("sre,sde->rd", grad_qkv, qkv_back, preferred_element_type=jnp.float32)

    grad_in = grad_sum(input_term, rows_here)
    grad_hidden_part, gain_zero, shift_zero = norm_back(hidden, ln_gain[0], ln_bias[0], grad_in)
    grad_hidden = grad_first + grad_hidden_part
    qkv_shard, out_shard, up_shard, down_shard = (
        lax.psum_scatter(qkv_grad, "dp", scatter_dimension=1, tiled=True),
        lax.psum_scatter(out_grad, "dp", scatter_dimension=1, tiled=True),
        lax.psum_scatter(up_grad, "dp", scatter_dimension=0, tiled=True),
        lax.psum_scatter(down_grad, "dp", scatter_dimension=1, tiled=True),
    )
    head_bias_qv, head_bias_one = lax.psum((bias_qv_grad, bias_one_grad), "dp")
    gain_stack = jnp.stack([gain_zero, gain_one, gain_two, gain_three])
    shift_stack = jnp.stack([shift_zero, shift_one, shift_two, shift_three])
    gain_total, offset_overall, bias_out_total, bias_two_total = lax.psum(
        (gain_stack, shift_stack, bias_out_grad, bias_two_grad), ("dp", "tensor")
    )
    output_rows, input_rows = (
        lax.all_to_all(result.astype(jnp.bfloat16), "dp", split_axis=0, concat_axis=0, tiled=True),
        lax.all_to_all(
            grad_hidden.astype(jnp.bfloat16), "dp", split_axis=0, concat_axis=0, tiled=True
        ),
    )
    return (
        output_rows,
        input_rows,
        qkv_shard,
        out_shard,
        up_shard,
        down_shard,
        head_bias_qv,
        bias_out_total,
        head_bias_one,
        bias_two_total,
        gain_total,
        offset_overall,
    )


def solution(mesh):
    placed = (
        P(("dp", "tensor"), None),
        P(("dp", "tensor"), None),
        P(),
        P(),
        P(None, "dp", "tensor"),
        P("tensor", "dp"),
        P("dp", "tensor"),
        P("tensor", "dp"),
        P(None, "tensor"),
        P(),
        P("tensor"),
        P(),
        P(),
        P(),
    )
    return jax.shard_map(
        body,
        mesh=mesh,
        in_specs=placed,
        out_specs=(
            P(("dp", "tensor"), None),
            P(("dp", "tensor"), None),
            P(None, "dp", "tensor"),
            P("tensor", "dp"),
            P("dp", "tensor"),
            P("tensor", "dp"),
            P(None, "tensor"),
            P(),
            P("tensor"),
            P(),
            P(),
            P(),
        ),
        check_vma=False,
    )
```

profile of v0, /device:TPU:0, one launch (start us, length us, event | category | flops | bytes accessed | tf_op | source)
XLA Modules:
  0.0 1348.8 jit_solution(9678845861428645542)
XLA Ops:
  14.7 13.3 all-to-all-done
  34.0 10.9 all_gather.30
  45.3 82.9 %all-gather.8.cloned.1.call-done = bf16[2048,1024]{1,0:T(8,128)(2,1)} async-done(((bf16[512,1024]{1,0:T(8,128)(2,1)}), bf16[2048,1024]{1,0:T(8,128)(2,1)}) %all-gather.8.cloned.1.call-update) | async-done | bytes 4194320 | tf_op jit(solution)/shard_map/all_gather | solution.py:36
  137.5 58.6 %while.32 = (s32[]{:T(128)}, bf16[4,512,4,64]{1,3,2,0:T(8,128)(2,1)}, f32[4,4,512,1]{2,1,3,0:T(4,128)S(1)}, f32[4,4,512,1]{2,1,3,0:T(4,128)S(1)}, s32[4]{0:T(128...) while((s32[]{:T(128)}, ...), condition=%wide.region_9.10_spmd, body=%wide.region_6.9_spmd.sunk | while | flops 851834880 | bytes 43106592 | solution.py:101
  204.2 74.6 %reduce-scatter.9.cloned.1.call-done = bf16[512,1024]{1,0:T(8,128)(2,1)} async-done(((bf16[2048,1024]{1,0:T(8,128)(2,1)}), bf16[512,1024]{1,0:T(8,128)(2,1)}) %reduce-scatter.9.cloned.1.call-update) | async-done | bytes 1048592 | tf_op jit(solution)/shard_map/reduce_scatter | solution.py:40
  286.5 22.6 %all-gather.14.cloned.1.call-done = bf16[1024,1024]{1,0:T(8,128)(2,1)} async-done(((bf16[128,1024]{1,0:T(8,128)(2,1)}), bf16[1024,1024]{1,0:T(8,128)(2,1)}) %all-gather.14.cloned.1.call-update) | async-done | bytes 2097168 | tf_op jit(solution)/shard_map/all_gather | solution.py:202
  309.1 82.9 %all-gather.12.cloned.1.call-done = bf16[2048,1024]{1,0:T(8,128)(2,1)} async-done(((bf16[512,1024]{1,0:T(8,128)(2,1)}), bf16[2048,1024]{1,0:T(8,128)(2,1)}) %all-gather.12.cloned.1.call-update) | async-done | bytes 4194320 | tf_op jit(solution)/shard_map/all_gather | solution.py:36
  392.0 26.2 %multiply_convert_fusion = (bf16[2048,1024]{1,0:T(8,128)(2,1)}, f32[2048,1024]{1,0:T(8,128)}, f32[2048,1024]{1,0:T(8,128)}) fusion(f32[1024]{0:T(1024)S(1)} %copy-done.58, bf16[2048,1024]{1,0:T(8,128)(2,1)} %all-gather.12.cloned.1.call-done, bf16[1024,1024]{1,0:T(8,128)(2,1)} %all-gather.14.cloned.1.call-done), kind=kOutput, calls=%fused_computation.69 | convolution fusion | flops 4433379328 | bytes 27267072 | tf_op jit(solution)/shard_map/dot_general | solution.py:205
  420.6 9.3 convolution_convert_fusion.2
  434.7 72.2 %reduce-scatter.11.cloned.1.call-done = bf16[512,1024]{1,0:T(8,128)(2,1)} async-done(((bf16[2048,1024]{1,0:T(8,128)(2,1)}), bf16[512,1024]{1,0:T(8,128)(2,1)}) %reduce-scatter.11.cloned.1.call-update) | async-done | bytes 1048592 | tf_op jit(solution)/shard_map/reduce_scatter | solution.py:40
  519.4 81.4 %all-gather.18.cloned.1.call-done = bf16[2048,1024]{1,0:T(8,128)(2,1)} async-done(((bf16[512,1024]{1,0:T(8,128)(2,1)}), bf16[2048,1024]{1,0:T(8,128)(2,1)}) %all-gather.18.cloned.1.call-update) | async-done | bytes 4194320 | tf_op jit(solution)/shard_map/all_gather | solution.py:49
  600.8 14.0 %convert_reduce_fusion = (f32[1024]{0:T(1024)}, bf16[2048,1024]{1,0:T(8,128)(2,1)S(1)}) fusion(f32[2048,1024]{1,0:T(8,128)} %get-tuple-element.431, f32[2048,1024]{1,0:T(8,128)} %get-tuple-element.460, f32[1024]{0:T(1024)S(1)} %copy-done.58, bf16[2048,1024]{1,0:T(8,128)(2,1)} %all-gather.18.cloned.1.call-done, ...), kind=kOutput, calls=%fused_computation.67 | convolution fusion | flops 4330617856 | bytes 27271168 | tf_op jit(solution)/shard_map/rd,fd->rf/dot_general | solution.py:224
  623.3 75.2 %reduce-scatter.13.cloned.1.call-done = bf16[512,1024]{1,0:T(8,128)(2,1)} async-done(((bf16[2048,1024]{1,0:T(8,128)(2,1)}), bf16[512,1024]{1,0:T(8,128)(2,1)}) %reduce-scatter.13.cloned.1.call-update) | async-done | bytes 1048592 | tf_op jit(solution)/shard_map/reduce_scatter | solution.py:53
  713.9 81.4 %all-gather.20.cloned.1.call-done = bf16[2048,1024]{1,0:T(8,128)(2,1)} async-done(((bf16[512,1024]{1,0:T(8,128)(2,1)}), bf16[2048,1024]{1,0:T(8,128)(2,1)}) %all-gather.20.cloned.1.call-update) | async-done | bytes 4194320 | tf_op jit(solution)/shard_map/all_gather | solution.py:49
  803.7 238.9 %while.33 = (s32[]{:T(128)}, f32[3072,4,64]{0,2,1:T(8,128)}, f32[3072,4,64]{0,2,1:T(8,128)}, bf16[4,512,4,64]{1,3,2,0:T(8,128)(2,1)}, s32[4]{0:T(128)S(1)}, /*in...) while((s32[]{:T(128)}, f32[3072,4,64]{0,2,1:T(8,128)}, ...), condition=%wide.region_36.37_spmd, body=%wide.region_34.36_spmd.sunk | while | flops 2073568256 | bytes 206397872 | solution.py:148
  824.9 18.0 %fusion.211 = bf16[4,512,4,64]{1,3,2,0:T(8,128)(2,1)} fusion(bf16[4,512,4,64]{1,3,2,0:T(8,128)(2,1)} %get-tuple-element.686, s32[]{:T(128)S(6)} %copy.78, f32[4,512,1536]{2,1,0:T(8,128)} %fusion.208, f32[4,512,1536]{2,1,0:T(8,128)} %copy-done, pred[512,1536]{1,0:T(8,128)(4,1)S(1)} %compare_and_fusion.5, ...), kind=kOutput, calls=%fused_computation.42.clone.1 | convolution fusion | flops 421662208 | bytes 52428808 | tf_op jit(solution)/shard_map/while/body/eval_jaxpr/hqk,khd->qhd/dot_general | solution.py:133
  842.9 20.6 %fusion.209 = f32[3072,4,64]{0,2,1:T(8,128)} fusion(f32[3072,4,64]{0,2,1:T(8,128)} %get-tuple-element.684, s32[]{:T(128)S(6)} %select_n.214, f32[4,512,1536]{2,1,0:T(8,128)} %fusion.208, f32[4,512,1536]{2,1,0:T(8,128)} %copy-done, pred[512,1536]{1,0:T(8,128)(4,1)S(1)} %compare_and_fusion.5, bf16[2048,4,64]{0,2,1:T(8,128)(2,1)} %get-tuple-element.708, ...), kind=kOutput, calls=%fused_computation.36.clone.1 | convolution fusion | flops 422317568 | bytes 54525960 | tf_op jit(solution)/shard_map/while/body/eval_jaxpr/hqk,qhd->khd/dot_general | solution.py:137
  884.5 18.1 %fusion.211 = bf16[4,512,4,64]{1,3,2,0:T(8,128)(2,1)} fusion(bf16[4,512,4,64]{1,3,2,0:T(8,128)(2,1)} %get-tuple-element.686, s32[]{:T(128)S(6)} %copy.78, f32[4,512,1536]{2,1,0:T(8,128)} %fusion.208, f32[4,512,1536]{2,1,0:T(8,128)} %copy-done, pred[512,1536]{1,0:T(8,128)(4,1)S(1)} %compare_and_fusion.5, ...), kind=kOutput, calls=%fused_computation.42.clone.1 | convolution fusion | flops 421662208 | bytes 52428808 | tf_op jit(solution)/shard_map/while/body/eval_jaxpr/hqk,khd->qhd/dot_general | solution.py:133
  902.6 20.5 %fusion.209 = f32[3072,4,64]{0,2,1:T(8,128)} fusion(f32[3072,4,64]{0,2,1:T(8,128)} %get-tuple-element.684, s32[]{:T(128)S(6)} %select_n.214, f32[4,512,1536]{2,1,0:T(8,128)} %fusion.208, f32[4,512,1536]{2,1,0:T(8,128)} %copy-done, pred[512,1536]{1,0:T(8,128)(4,1)S(1)} %compare_and_fusion.5, bf16[2048,4,64]{0,2,1:T(8,128)(2,1)} %get-tuple-element.708, ...), kind=kOutput, calls=%fused_computation.36.clone.1 | convolution fusion | flops 422317568 | bytes 54525960 | tf_op jit(solution)/shard_map/while/body/eval_jaxpr/hqk,qhd->khd/dot_general | solution.py:137
  944.1 18.1 %fusion.211 = bf16[4,512,4,64]{1,3,2,0:T(8,128)(2,1)} fusion(bf16[4,512,4,64]{1,3,2,0:T(8,128)(2,1)} %get-tuple-element.686, s32[]{:T(128)S(6)} %copy.78, f32[4,512,1536]{2,1,0:T(8,128)} %fusion.208, f32[4,512,1536]{2,1,0:T(8,128)} %copy-done, pred[512,1536]{1,0:T(8,128)(4,1)S(1)} %compare_and_fusion.5, ...), kind=kOutput, calls=%fused_computation.42.clone.1 | convolution fusion | flops 421662208 | bytes 52428808 | tf_op jit(solution)/shard_map/while/body/eval_jaxpr/hqk,khd->qhd/dot_general | solution.py:133
  962.2 20.5 %fusion.209 = f32[3072,4,64]{0,2,1:T(8,128)} fusion(f32[3072,4,64]{0,2,1:T(8,128)} %get-tuple-element.684, s32[]{:T(128)S(6)} %select_n.214, f32[4,512,1536]{2,1,0:T(8,128)} %fusion.208, f32[4,512,1536]{2,1,0:T(8,128)} %copy-done, pred[512,1536]{1,0:T(8,128)(4,1)S(1)} %compare_and_fusion.5, bf16[2048,4,64]{0,2,1:T(8,128)(2,1)} %get-tuple-element.708, ...), kind=kOutput, calls=%fused_computation.36.clone.1 | convolution fusion | flops 422317568 | bytes 54525960 | tf_op jit(solution)/shard_map/while/body/eval_jaxpr/hqk,qhd->khd/dot_general | solution.py:137
  1003.6 18.1 %fusion.211 = bf16[4,512,4,64]{1,3,2,0:T(8,128)(2,1)} fusion(bf16[4,512,4,64]{1,3,2,0:T(8,128)(2,1)} %get-tuple-element.686, s32[]{:T(128)S(6)} %copy.78, f32[4,512,1536]{2,1,0:T(8,128)} %fusion.208, f32[4,512,1536]{2,1,0:T(8,128)} %copy-done, pred[512,1536]{1,0:T(8,128)(4,1)S(1)} %compare_and_fusion.5, ...), kind=kOutput, calls=%fused_computation.42.clone.1 | convolution fusion | flops 421662208 | bytes 52428808 | tf_op jit(solution)/shard_map/while/body/eval_jaxpr/hqk,khd->qhd/dot_general | solution.py:133
  1021.7 20.4 %fusion.209 = f32[3072,4,64]{0,2,1:T(8,128)} fusion(f32[3072,4,64]{0,2,1:T(8,128)} %get-tuple-element.684, s32[]{:T(128)S(6)} %select_n.214, f32[4,512,1536]{2,1,0:T(8,128)} %fusion.208, f32[4,512,1536]{2,1,0:T(8,128)} %copy-done, pred[512,1536]{1,0:T(8,128)(4,1)S(1)} %compare_and_fusion.5, bf16[2048,4,64]{0,2,1:T(8,128)(2,1)} %get-tuple-element.708, ...), kind=kOutput, calls=%fused_computation.36.clone.1 | convolution fusion | flops 422317568 | bytes 54525960 | tf_op jit(solution)/shard_map/while/body/eval_jaxpr/hqk,qhd->khd/dot_general | solution.py:137
  1068.0 10.0 fusion.154
  1078.3 10.0 fusion.155
  1098.0 37.9 %reduce-scatter.15.cloned.1.call-done = bf16[512,1024]{1,0:T(8,128)(2,1)} async-done(((bf16[2048,1024]{1,0:T(8,128)(2,1)}), bf16[512,1024]{1,0:T(8,128)(2,1)}) %reduce-scatter.15.cloned.1.call-update) | async-done | bytes 1048592 | tf_op jit(solution)/shard_map/reduce_scatter | solution.py:53
  1150.5 20.3 %all-reduce.4 = (f32[2,256]{1,0:T(2,128)}, f32[1024]{0:T(1024)}) all-reduce(f32[2,256]{1,0:T(2,128)S(1)} %pad_maximum_fusion.3, f32[1024]{0:T(1024)S(1)} %copy-done.55), channel_id=1, replica_groups=mesh['dp'=8,'tensor'=4] {'dp'}, use_global_device_ids=true, to_apply=%region_48.49 | all-reduce | flops 1536 | bytes 12288 | tf_op jit(solution)/shard_map/psum | solution.py:279
  1170.9 15.4 %reduce-scatter.17.cloned.1.call-done = f32[3,128,256]{1,2,0:T(8,128)} async-done(((f32[3,1024,256]{1,2,0:T(8,128)}), f32[3,128,256]{1,2,0:T(8,128)}) %reduce-scatter.17.cloned.1.call-update) | async-done | bytes 393232 | tf_op jit(solution)/shard_map/reduce_scatter | solution.py:274
  1188.3 40.5 %all-reduce.3 = (f32[1024]{0:T(1024)}, f32[1024]{0:T(1024)}, f32[4,1024]{1,0:T(4,128)}, f32[4,1024]{1,0:T(4,128)}) all-reduce(f32[1024]{0:T(1024)S(1)} %copy-done.53, f32[1024]{0:T(1024)S(1)} %copy-done.52, f32[4,1024]{1,0:T(4,128)S(1)} %get-tuple-element.461, ...), channel_id=1, replica_groups=mesh['dp'=8,'tensor'=4] {'dp','tensor'}, use_global_device_ids=true, to_apply=%region_50.51 | all-reduce | flops 10240 | bytes 81920 | tf_op jit(solution)/shard_map/psum | solution.py:282
  1228.8 13.6 %reduce-scatter.21.cloned.1.call-done = f32[128,1024]{1,0:T(8,128)} async-done(((f32[1024,1024]{1,0:T(8,128)}), f32[128,1024]{1,0:T(8,128)}) %reduce-scatter.21.cloned.1.call-update) | async-done | bytes 524304 | tf_op jit(solution)/shard_map/reduce_scatter | solution.py:276
  1242.4 55.1 %reduce-scatter.23.cloned.1.call-done = f32[1024,128]{1,0:T(8,128)} async-done(((f32[1024,1024]{1,0:T(8,128)}), f32[1024,128]{1,0:T(8,128)}) %reduce-scatter.23.cloned.1.call-update) | async-done | bytes 524304 | tf_op jit(solution)/shard_map/reduce_scatter | solution.py:277
  1297.5 40.0 %reduce-scatter.19.cloned.1.call-done = f32[256,128]{1,0:T(8,128)} async-done(((f32[256,1024]{1,0:T(8,128)}), f32[256,128]{1,0:T(8,128)}) %reduce-scatter.19.cloned.1.call-update) | async-done | bytes 131088 | tf_op jit(solution)/shard_map/reduce_scatter | solution.py:275
  (362 shorter events, 275.9 us)
Async XLA Ops:
  7.2 20.7 %all-to-all-start = ((bf16[8,64,1024]{2,1,0:T(8,128)(2,1)}), bf16[8,64,1024]{2,1,0:T(8,128)(2,1)S(1)}, u32[]{:S(2)}, u32[]{:S(2)}) async-start(bf16[8,64,1024]{2,1,0:T(8,128)(2,1)} %bitcast.177), calls=%async_computation | async-start | bytes 2097152 | tf_op jit(solution)/shard_map/all_to_all | solution.py:163
  12.5 32.8 %all-gather.10.cloned.1.call-start = ((), (), s32[]{:S(2)}) async-start(), calls=%async_computation.13 | async-start | bytes 1769472 | tf_op jit(solution)/shard_map/all_gather | solution.py:177
  13.4 114.9 %all-gather.8.cloned.1.call-start = ((), (), s32[]{:S(2)}) async-start(), calls=%async_computation.12 | async-start | bytes 5242880 | tf_op jit(solution)/shard_map/all_gather | solution.py:36
  28.0 254.6 %copy-start.1 = (bf16[8,64,1024]{2,1,0:T(8,128)(2,1)}, bf16[8,64,1024]{2,1,0:T(8,128)(2,1)S(1)}, u32[]{:S(2)}) copy-start(bf16[8,64,1024]{2,1,0:T(8,128)(2,1)S(1)} %all-to-all-done) | copy-start | bytes 3145732
  30.3 103.7 %copy-start.39 = (f32[512]{0:T(512)}, f32[512]{0:T(512)S(1)}, u32[]{:S(2)}) copy-start(f32[512]{0:T(512)S(1)} %add.362) | copy-start | bytes 6148
  30.4 103.7 %copy-start.35 = (f32[512]{0:T(512)}, f32[512]{0:T(512)S(1)}, u32[]{:S(2)}) copy-start(f32[512]{0:T(512)S(1)} %rsqrt.44) | copy-start | bytes 6148
  33.1 245.6 %reduce-scatter.9.cloned.1.call-start = ((), (), s32[]{:S(2)}) async-start(), calls=%async_computation.14 | async-start | bytes 5242880 | tf_op jit(solution)/shard_map/reduce_scatter | solution.py:40
  44.8 154.3 %copy-start.20 = (bf16[256,1024]{1,0:T(8,128)(2,1)}, bf16[256,1024]{1,0:T(8,128)(2,1)S(1)}, u32[]{:S(2)}) copy-start(bf16[256,1024]{1,0:T(8,128)(2,1)S(1)} %all_gather.30) | copy-start | bytes 1572868
  203.3 75.5 %copy-start.22 = (f32[1024]{0:T(1024)S(1)}, f32[1024]{0:T(1024)}, u32[]{:S(2)}) copy-start(f32[1024]{0:T(1024)} %param.27) | copy-start | bytes 12292
  203.3 79.3 %copy-start.31 = (f32[1,1024]{1,0:T(1,128)S(1)}, f32[1,1024]{1,0:T(1,128)}, u32[]{:S(2)}) copy-start(f32[1,1024]{1,0:T(1,128)} %get-tuple-element.445) | copy-start | bytes 12292
  203.3 79.3 %copy-start.49 = (f32[1,1024]{1,0:T(1,128)S(1)}, f32[1,1024]{1,0:T(1,128)}, u32[]{:S(2)}) copy-start(f32[1,1024]{1,0:T(1,128)} %get-tuple-element.449) | copy-start | bytes 12292
  203.3 105.8 %all-gather.14.cloned.1.call-start = ((), (), s32[]{:S(2)}) async-start(), calls=%async_computation.16 | async-start | bytes 2359296 | tf_op jit(solution)/shard_map/all_gather | solution.py:202
  203.9 188.0 %all-gather.12.cloned.1.call-start = ((), (), s32[]{:S(2)}) async-start(), calls=%async_computation.15 | async-start | bytes 5242880 | tf_op jit(solution)/shard_map/all_gather | solution.py:36
  284.4 107.6 %copy-start.58 = (f32[1024]{0:T(1024)S(1)}, f32[1024]{0:T(1024)}, u32[]{:S(2)}) copy-start(f32[1024]{0:T(1024)} %param.28) | copy-start | bytes 12292
  285.9 134.7 %all-gather.16.cloned.1.call-start = ((), (), s32[]{:S(2)}) async-start(), calls=%async_computation.17 | async-start | bytes 2359296 | tf_op jit(solution)/shard_map/all_gather | solution.py:203
  286.4 220.4 %reduce-scatter.11.cloned.1.call-start = ((), (), s32[]{:S(2)}) async-start(), calls=%async_computation.18 | async-start | bytes 5242880 | tf_op jit(solution)/shard_map/reduce_scatter | solution.py:40
  429.9 76.9 %copy-start.23 = (f32[1024]{0:T(1024)S(1)}, f32[1024]{0:T(1024)}, u32[]{:S(2)}) copy-start(f32[1024]{0:T(1024)} %param.29) | copy-start | bytes 12292
  430.0 80.7 %all-to-all-start.2 = ((bf16[8,64,1024]{2,1,0:T(8,128)(2,1)}), bf16[8,64,1024]{2,1,0:T(8,128)(2,1)}, u32[]{:S(2)}, u32[]{:S(2)}) async-start(bf16[8,64,1024]{2,1,0:T(8,128)(2,1)} %bitcast.31), calls=%async_computation.4 | async-start | bytes 2097152 | tf_op jit(solution)/shard_map/all_to_all | solution.py:164
  434.2 76.5 %copy-start.33 = (f32[1,1024]{1,0:T(1,128)S(1)}, f32[1,1024]{1,0:T(1,128)}, u32[]{:S(2)}) copy-start(f32[1,1024]{1,0:T(1,128)} %get-tuple-element.447) | copy-start | bytes 12292
  434.2 166.6 %all-gather.18.cloned.1.call-start = ((), (), s32[]{:S(2)}) async-start(), calls=%async_computation.19 | async-start | bytes 5242880 | tf_op jit(solution)/shard_map/all_gather | solution.py:49
  519.4 179.2 %reduce-scatter.13.cloned.1.call-start = ((), (), s32[]{:S(2)}) async-start(), calls=%async_computation.20 | async-start | bytes 5242880 | tf_op jit(solution)/shard_map/reduce_scatter | solution.py:53
  623.1 172.1 %all-gather.20.cloned.1.call-start = ((), (), s32[]{:S(2)}) async-start(), calls=%async_computation.21 | async-start | bytes 5242880 | tf_op jit(solution)/shard_map/all_gather | solution.py:49
  711.2 84.1 %copy-start.21 = (bf16[256,1024]{1,0:T(8,128)(2,1)S(1)}, bf16[256,1024]{1,0:T(8,128)(2,1)}, u32[]{:S(2)}) copy-start(bf16[256,1024]{1,0:T(8,128)(2,1)} %copy-done.20) | copy-start | bytes 1572868
  713.8 422.1 %reduce-scatter.15.cloned.1.call-start = ((), (), s32[]{:S(2)}) async-start(), calls=%async_computation.22 | async-start | bytes 5242880 | tf_op jit(solution)/shard_map/reduce_scatter | solution.py:53
  1060.5 125.8 %reduce-scatter.17.cloned.1.call-start = ((), (), s32[]{:S(2)}) async-start(), calls=%async_computation.23 | async-start | bytes 3538944 | tf_op jit(solution)/shard_map/reduce_scatter | solution.py:274
  1068.0 174.4 %reduce-scatter.21.cloned.1.call-start = ((), (), s32[]{:S(2)}) async-start(), calls=%async_computation.25 | async-start | bytes 4718592 | tf_op jit(solution)/shard_map/reduce_scatter | solution.py:276
  1078.0 219.5 %reduce-scatter.23.cloned.1.call-start = ((), (), s32[]{:S(2)}) async-start(), calls=%async_computation.26 | async-start | bytes 4718592 | tf_op jit(solution)/shard_map/reduce_scatter | solution.py:277
  1089.0 54.4 %all-to-all-start.1 = ((bf16[8,64,1024]{2,1,0:T(8,128)(2,1)}), bf16[8,64,1024]{2,1,0:T(8,128)(2,1)}, u32[]{:S(2)}, u32[]{:S(2)}) async-start(bf16[8,64,1024]{2,1,0:T(8,128)(2,1)} %bitcast.29), calls=%async_computation.3 | async-start | bytes 2097152 | tf_op jit(solution)/shard_map/all_to_all | solution.py:286
  1093.3 42.6 %copy-start.2 = (bf16[8,64,1024]{2,1,0:T(8,128)(2,1)S(1)}, bf16[8,64,1024]{2,1,0:T(8,128)(2,1)}, u32[]{:S(2)}) copy-start(bf16[8,64,1024]{2,1,0:T(8,128)(2,1)} %copy-done.1) | copy-start | bytes 3145732
  1093.3 42.6 %copy-start.26 = (f32[1,1024]{1,0:T(1,128)S(1)}, f32[1,1024]{1,0:T(1,128)}, u32[]{:S(2)}) copy-start(f32[1,1024]{1,0:T(1,128)} %copy-done.25) | copy-start | bytes 12292
  1093.3 244.2 %reduce-scatter.19.cloned.1.call-start = ((), (), s32[]{:S(2)}) async-start(), calls=%async_computation.24 | async-start | bytes 1179648 | tf_op jit(solution)/shard_map/reduce_scatter | solution.py:275
  1143.4 85.4 %all-to-all-start.3 = ((bf16[8,64,1024]{2,1,0:T(8,128)(2,1)}), bf16[8,64,1024]{2,1,0:T(8,128)(2,1)}, u32[]{:S(2)}, u32[]{:S(2)}) async-start(bf16[8,64,1024]{2,1,0:T(8,128)(2,1)} %bitcast.172), calls=%async_computation.7 | async-start | bytes 2097152 | tf_op jit(solution)/shard_map/all_to_all | solution.py:287
  (55 other events, 670.8 us)
Sparse Core Ops, SparseCore 0:
  15.8 29.4 all-gather.9
  47.5 80.7 all-gather.7
  203.4 75.2 reduce-scatter.8
  280.6 28.4 all-gather.13
  311.2 80.7 all-gather.11
  393.8 26.7 all-gather.15
  430.1 76.7 reduce-scatter.10
  519.5 81.2 all-gather.17
  623.2 75.2 reduce-scatter.12
  713.9 81.2 all-gather.19
  1060.6 75.2 reduce-scatter.14
  1139.2 47.0 reduce-scatter.16
  1190.6 51.7 reduce-scatter.20
  1246.1 51.3 reduce-scatter.22
  1301.4 36.0 reduce-scatter.18
where the time goes:
time: 1350 us
  waiting for transfers between devices  753 us (56%)
  matrix products  364 us (27%)
  blocking collectives  71.8 us (5%)
  other arithmetic  71 us (5%)
  local copies, waits for them, and re-layouts  40.9 us (3%)
  starting transfers between devices  19.8 us (1%)
  between operations  15 us (1%)
  loops' own time  13.9 us (1%)
    all_gather x2, waiting for transfers between devices, lane_gather(): return lax.all_gather(rows_low, 'tensor', axis=0, tiled=True)  166 us
    all_gather x2, waiting for transfers between devices, grad_gather(): return lax.all_gather(rows_low, 'tensor', axis=0, tiled=True)  163 us
    reduce_scatter x2, waiting for transfers between devices, lane_sum(): lax.psum_scatter(term_fn(jnp.int32(0), rows_here * lax.axis_size('tensor'...  147 us
    reduce_scatter x2, waiting for transfers between devices, grad_sum(): lax.psum_scatter(term_fn(jnp.int32(0), rows_here * lax.axis_size('tensor'...  113 us
    dot_general x4, matrix products, one_step(): jnp.einsum('hqk,qhd->khd', grad_score, query_block, preferred_element_typ...  82 us
    dot_general x4, matrix products, one_step(): jnp.einsum('hqk,khd->qhd', grad_score, key_block, preferred_element_type=...  72.3 us
    reduce_scatter x1, waiting for transfers between devices, body(): lax.psum_scatter(down_grad, 'dp', scatter_dimension=1, tiled=True)  55.1 us
    psum x1, blocking collectives, body(): lax.psum((gain_stack, shift_stack, bias_out_grad, bias_two_grad), ('dp',...  40.5 us
  transfers between devices with their start and end apart: 19, of which 16 were waited for; matrix products, arithmetic and copies ran while one was open for 7% of the time, Pallas kernels for 0%

commit v1 on v0

--- a/solution.py
+++ b/solution.py
@@ -4,6 +4,7 @@
 import jax.numpy as jnp
 from jax import lax
 from jax.sharding import PartitionSpec as P
+from jax.lax import axis_index, axis_size, ppermute
 
 DH = 64
 MAXLEN = 1024
@@ -13,6 +14,21 @@
 MASKED_OUT = -1000000000.0
 
 
+def connect_cubes_now(local_x):
+    heard = axis_size("tensor")
+    finding = axis_index("tensor")
+    view_out, y_new = (heard, finding)
+    p_next, item_now = (local_x, 1)
+    while item_now < view_out:
+        carry_out = tuple(((dev_i, dev_i ^ item_now) for dev_i in range(view_out)))
+        r_now = ppermute(p_next, "tensor", carry_out)
+        then = jnp.concatenate([p_next, r_now], 0)
+        r2 = jnp.concatenate([r_now, p_next], 0)
+        p_next = jnp.where(y_new & item_now == 0, then, r2)
+        item_now = 2 * item_now
+    return p_next
+
+
 def scaled_norm(values, norm_gain, norm_shift):
     peak = jnp.max(jnp.abs(values), axis=-1, keepdims=True) + NORM_EPS
     scaled = values / peak
@@ -33,7 +49,7 @@
 
 
 def lane_gather(rows_low):
-    return lax.all_gather(rows_low, "tensor", axis=0, tiled=True)
+    return connect_cubes_now(rows_low)
 
 
 def lane_sum(term_fn, rows_here):

time: 1350 us -> 1400 us (1.037)
  matrix products: 364 us -> 343 us
  local copies, waits for them, and re-layouts: 40.9 us -> 60.5 us
  waiting for transfers between devices: 753 us -> 772 us
    ppermute x0 -> x4, waiting for transfers between devices: none -> 206 us  [connect_cubes_now(): r_now = ppermute(p_next, 'tensor', carry_out)]
    all_gather x2 -> x0, waiting for transfers between devices: 166 us -> none  [lane_gather(): return lax.all_gather(rows_low, 'tensor', axis=0, tiled=True)]
    reduce_scatter x1, waiting for transfers between devices: 13.6 us -> 55.1 us  [body(): lax.psum_scatter(up_grad, 'dp', scatter_dimension=0, tiled=True)]
    reduce_scatter x1, waiting for transfers between devices: 55.1 us -> 13.6 us  [body(): lax.psum_scatter(down_grad, 'dp', scatter_dimension=1, tiled=True)]
    all_gather x1, waiting for transfers between devices: 22.6 us -> 0.02 us  [body(): lax.all_gather(w_1, 'dp', axis=0, tiled=True)]
    while x16 -> x32, local copies, waits for them, and re-layouts: 0.47 us -> 16.8 us
    dot_general x4, matrix products: 20.4 us -> 5.61 us  [one_step(): jnp.einsum('hqk,qhd->khd', prob_low, grad_block, preferred_element_type=j...]
  transfers between devices with their start and end apart: 19 -> 21, of which waited for: 16 -> 15; matrix products, arithmetic and copies ran while one was open for 7% -> 7% of each run, Pallas kernels for 0% -> 0%
where the time goes in v1:
time: 1400 us; the launch traced here: 1390 us
  waiting for transfers between devices  772 us (55%)
  matrix products  343 us (24%)
  other arithmetic  82.4 us (6%)
  blocking collectives  73.9 us (5%)
  local copies, waits for them, and re-layouts  60.5 us (4%)
  starting transfers between devices  28.4 us (2%)
  between operations  14.9 us (1%)
    ppermute x4, waiting for transfers between devices, connect_cubes_now(): r_now = ppermute(p_next, 'tensor', carry_out)  206 us
    all_gather x2, waiting for transfers between devices, grad_gather(): return lax.all_gather(rows_low, 'tensor', axis=0, tiled=True)  163 us
    reduce_scatter x2, waiting for transfers between devices, lane_sum(): lax.psum_scatter(term_fn(jnp.int32(0), rows_here * lax.axis_size('tensor'...  154 us
    reduce_scatter x2, waiting for transfers between devices, grad_sum(): lax.psum_scatter(term_fn(jnp.int32(0), rows_here * lax.axis_size('tensor'...  110 us
    dot_general x4, matrix products, one_step(): jnp.einsum('hqk,qhd->khd', grad_score, query_block, preferred_element_typ...  77 us
    dot_general x4, matrix products, one_step(): jnp.einsum('hqk,khd->qhd', grad_score, key_block, preferred_element_type=...  73.3 us
    reduce_scatter x1, waiting for transfers between devices, body(): lax.psum_scatter(up_grad, 'dp', scatter_dimension=0, tiled=True)  55.1 us
    psum x1, blocking collectives, body(): lax.psum((gain_stack, shift_stack, bias_out_grad, bias_two_grad), ('dp',...  40.5 us
  transfers between devices with their start and end apart: 21, of which 15 were waited for; matrix products, arithmetic and copies ran while one was open for 7% of the time, Pallas kernels for 0%

profile of v1, /device:TPU:0, one launch (start us, length us, event | category | flops | bytes accessed | tf_op | source)
XLA Modules:
  0.0 1389.4 jit_solution(10514000678118401020)
XLA Ops:
  13.8 14.1 %all-to-all-done = bf16[8,64,1024]{2,1,0:T(8,128)(2,1)S(1)} async-done(((bf16[8,64,1024]{2,1,0:T(8,128)(2,1)}), bf16[8,64,1024]{2,1,0:T(8,128)(2,1)S(1)}, u32[]{:S(2)}, u32[]{:S(2)}) %all-to-all-start) | async-done | bytes 1048608 | tf_op jit(solution)/shard_map/all_to_all | solution.py:179
  35.2 19.6 %collective-permute-done = bf16[512,1024]{1,0:T(8,128)(2,1)S(1)} collective-permute-done((bf16[512,1024]{1,0:T(8,128)(2,1)S(1)}, bf16[512,1024]{1,0:T(8,128)(2,1)S(1)}, u32[]{:S(2)}, u32[]{:S(2)}) %collective-permute-start) | collective-permute-done | bytes 1048608 | tf_op jit(solution)/shard_map/ppermute | solution.py:24
  60.5 13.0 all_gather.23
  73.5 73.4 %collective-permute-done.1 = bf16[1024,1024]{1,0:T(8,128)(2,1)S(1)} collective-permute-done((bf16[1024,1024]{1,0:T(8,128)(2,1)}, bf16[1024,1024]{1,0:T(8,128)(2,1)S(1)}, u32[]{:S(2)}, u32[]{:S(2)}) %collective-permute-start.1) | collective-permute-done | bytes 2097184 | tf_op jit(solution)/shard_map/ppermute | solution.py:24
  155.9 57.8 %while.32 = (s32[]{:T(128)}, bf16[4,512,4,64]{1,3,2,0:T(8,128)(2,1)}, f32[4,4,512,1]{2,1,3,0:T(4,128)S(1)}, f32[4,4,512,1]{2,1,3,0:T(4,128)S(1)}, s32[4]{0:T(128...) while((s32[]{:T(128)}, ...), condition=%wide.region_9.10_spmd, body=%wide.region_6.9_spmd.sunk | while | flops 851834880 | bytes 43106592 | solution.py:117
  222.1 81.3 %reduce-scatter.9.cloned.1.call-done = bf16[512,1024]{1,0:T(8,128)(2,1)} async-done(((bf16[2048,1024]{1,0:T(8,128)(2,1)}), bf16[512,1024]{1,0:T(8,128)(2,1)}) %reduce-scatter.9.cloned.1.call-update) | async-done | bytes 1048592 | tf_op jit(solution)/shard_map/reduce_scatter | solution.py:56
  311.1 23.4 %collective-permute-done.2 = bf16[512,1024]{1,0:T(8,128)(2,1)S(1)} collective-permute-done((bf16[512,1024]{1,0:T(8,128)(2,1)S(1)}, bf16[512,1024]{1,0:T(8,128)(2,1)S(1)}, u32[]{:S(2)}, u32[]{:S(2)}) %collective-permute-start.2) | collective-permute-done | bytes 1048608 | tf_op jit(solution)/shard_map/ppermute | solution.py:24
  340.0 90.0 %collective-permute-done.3 = bf16[1024,1024]{1,0:T(8,128)(2,1)} collective-permute-done((bf16[1024,1024]{1,0:T(8,128)(2,1)}, bf16[1024,1024]{1,0:T(8,128)(2,1)}, u32[]{:S(2)}, u32[]{:S(2)}) %collective-permute-start.3) | collective-permute-done | bytes 2097184 | tf_op jit(solution)/shard_map/ppermute | solution.py:24
  429.9 28.0 %multiply_convert_fusion = (bf16[2048,1024]{1,0:T(8,128)(2,1)}, f32[2048,1024]{1,0:T(8,128)}, f32[2048,1024]{1,0:T(8,128)}) fusion(f32[1024]{0:T(1024)S(1)} %copy-done.60, bf16[1024,1024]{1,0:T(8,128)(2,1)} %all-gather.8.cloned.1.call-done, bf16[1024,1024]{1,0:T(8,128)(2,1)} %collective-permute-done.3, bf16[1024,1024]{1,0:T(8,128)(2,1)} %maximum_select_fusion.3, ...), kind=kOutput, calls=%fused_computation.69 | convolution fusion | flops 4452253696 | bytes 27267072 | tf_op jit(solution)/shard_map/dot_general | solution.py:221
  458.0 9.3 convolution_convert_fusion.2
  472.0 72.3 %reduce-scatter.11.cloned.1.call-done = bf16[512,1024]{1,0:T(8,128)(2,1)} async-done(((bf16[2048,1024]{1,0:T(8,128)(2,1)}), bf16[512,1024]{1,0:T(8,128)(2,1)}) %reduce-scatter.11.cloned.1.call-update) | async-done | bytes 1048592 | tf_op jit(solution)/shard_map/reduce_scatter | solution.py:56
  556.9 81.4 %all-gather.12.cloned.1.call-done = bf16[2048,1024]{1,0:T(8,128)(2,1)} async-done(((bf16[512,1024]{1,0:T(8,128)(2,1)}), bf16[2048,1024]{1,0:T(8,128)(2,1)}) %all-gather.12.cloned.1.call-update) | async-done | bytes 4194320 | tf_op jit(solution)/shard_map/all_gather | solution.py:65
  662.5 75.2 %reduce-scatter.13.cloned.1.call-done = bf16[512,1024]{1,0:T(8,128)(2,1)} async-done(((bf16[2048,1024]{1,0:T(8,128)(2,1)}), bf16[512,1024]{1,0:T(8,128)(2,1)}) %reduce-scatter.13.cloned.1.call-update) | async-done | bytes 1048592 | tf_op jit(solution)/shard_map/reduce_scatter | solution.py:69
  752.8 81.4 %all-gather.14.cloned.1.call-done = bf16[2048,1024]{1,0:T(8,128)(2,1)} async-done(((bf16[512,1024]{1,0:T(8,128)(2,1)}), bf16[2048,1024]{1,0:T(8,128)(2,1)}) %all-gather.14.cloned.1.call-update) | async-done | bytes 4194320 | tf_op jit(solution)/shard_map/all_gather | solution.py:65
  841.0 236.4 %while.33 = (s32[]{:T(128)}, f32[3072,4,64]{0,2,1:T(8,128)}, f32[3072,4,64]{0,2,1:T(8,128)S(1)}, bf16[4,512,4,64]{1,3,2,0:T(8,128)(2,1)}, s32[4]{0:T(128)S(1)}, ...) while((s32[]{:T(128)}, f32[3072,4,64]{0,2,1:T(8,128)}, ...), condition=%wide.region_36.37_spmd, body=%wide.region_34.36_spmd.sunk | while | flops 2073568256 | bytes 215835120 | solution.py:164
  862.7 18.4 %fusion.212 = bf16[4,512,4,64]{1,3,2,0:T(8,128)(2,1)} fusion(bf16[4,512,4,64]{1,3,2,0:T(8,128)(2,1)} %get-tuple-element.686, s32[]{:T(128)S(6)} %copy.78, f32[4,512,1536]{2,1,0:T(8,128)} %fusion.209, f32[4,512,1536]{2,1,0:T(8,128)} %copy-done, pred[512,1536]{1,0:T(8,128)(4,1)} %copy-done.7, bf16[3072,4,64]{0,2,1:T(8,128)(2,1)} %get-tuple-element.711, ...), kind=kOutput, calls=%fused_computation.42.clone.1 | convolution fusion | flops 421662208 | bytes 52428808 | tf_op jit(solution)/shard_map/while/body/eval_jaxpr/hqk,khd->qhd/dot_general | solution.py:149
  881.1 19.2 %fusion.210 = f32[3072,4,64]{0,2,1:T(8,128)} fusion(f32[3072,4,64]{0,2,1:T(8,128)} %get-tuple-element.684, s32[]{:T(128)S(6)} %select_n.270, f32[4,512,1536]{2,1,0:T(8,128)} %fusion.209, f32[4,512,1536]{2,1,0:T(8,128)} %copy-done, pred[512,1536]{1,0:T(8,128)(4,1)} %copy-done.7, bf16[2048,4,64]{0,2,1:T(8,128)(2,1)} %get-tuple-element.708, ...), kind=kOutput, calls=%fused_computation.36.clone.1 | convolution fusion | flops 422317568 | bytes 54525960 | tf_op jit(solution)/shard_map/while/body/eval_jaxpr/hqk,qhd->khd/dot_general | solution.py:153
  921.8 18.3 %fusion.212 = bf16[4,512,4,64]{1,3,2,0:T(8,128)(2,1)} fusion(bf16[4,512,4,64]{1,3,2,0:T(8,128)(2,1)} %get-tuple-element.686, s32[]{:T(128)S(6)} %copy.78, f32[4,512,1536]{2,1,0:T(8,128)} %fusion.209, f32[4,512,1536]{2,1,0:T(8,128)} %copy-done, pred[512,1536]{1,0:T(8,128)(4,1)} %copy-done.7, bf16[3072,4,64]{0,2,1:T(8,128)(2,1)} %get-tuple-element.711, ...), kind=kOutput, calls=%fused_computation.42.clone.1 | convolution fusion | flops 421662208 | bytes 52428808 | tf_op jit(solution)/shard_map/while/body/eval_jaxpr/hqk,khd->qhd/dot_general | solution.py:149
  940.2 19.2 %fusion.210 = f32[3072,4,64]{0,2,1:T(8,128)} fusion(f32[3072,4,64]{0,2,1:T(8,128)} %get-tuple-element.684, s32[]{:T(128)S(6)} %select_n.270, f32[4,512,1536]{2,1,0:T(8,128)} %fusion.209, f32[4,512,1536]{2,1,0:T(8,128)} %copy-done, pred[512,1536]{1,0:T(8,128)(4,1)} %copy-done.7, bf16[2048,4,64]{0,2,1:T(8,128)(2,1)} %get-tuple-element.708, ...), kind=kOutput, calls=%fused_computation.36.clone.1 | convolution fusion | flops 422317568 | bytes 54525960 | tf_op jit(solution)/shard_map/while/body/eval_jaxpr/hqk,qhd->khd/dot_general | solution.py:153
  980.9 18.3 %fusion.212 = bf16[4,512,4,64]{1,3,2,0:T(8,128)(2,1)} fusion(bf16[4,512,4,64]{1,3,2,0:T(8,128)(2,1)} %get-tuple-element.686, s32[]{:T(128)S(6)} %copy.78, f32[4,512,1536]{2,1,0:T(8,128)} %fusion.209, f32[4,512,1536]{2,1,0:T(8,128)} %copy-done, pred[512,1536]{1,0:T(8,128)(4,1)} %copy-done.7, bf16[3072,4,64]{0,2,1:T(8,128)(2,1)} %get-tuple-element.711, ...), kind=kOutput, calls=%fused_computation.42.clone.1 | convolution fusion | flops 421662208 | bytes 52428808 | tf_op jit(solution)/shard_map/while/body/eval_jaxpr/hqk,khd->qhd/dot_general | solution.py:149
  999.2 19.2 %fusion.210 = f32[3072,4,64]{0,2,1:T(8,128)} fusion(f32[3072,4,64]{0,2,1:T(8,128)} %get-tuple-element.684, s32[]{:T(128)S(6)} %select_n.270, f32[4,512,1536]{2,1,0:T(8,128)} %fusion.209, f32[4,512,1536]{2,1,0:T(8,128)} %copy-done, pred[512,1536]{1,0:T(8,128)(4,1)} %copy-done.7, bf16[2048,4,64]{0,2,1:T(8,128)(2,1)} %get-tuple-element.708, ...), kind=kOutput, calls=%fused_computation.36.clone.1 | convolution fusion | flops 422317568 | bytes 54525960 | tf_op jit(solution)/shard_map/while/body/eval_jaxpr/hqk,qhd->khd/dot_general | solution.py:153
  1039.9 18.2 %fusion.212 = bf16[4,512,4,64]{1,3,2,0:T(8,128)(2,1)} fusion(bf16[4,512,4,64]{1,3,2,0:T(8,128)(2,1)} %get-tuple-element.686, s32[]{:T(128)S(6)} %copy.78, f32[4,512,1536]{2,1,0:T(8,128)} %fusion.209, f32[4,512,1536]{2,1,0:T(8,128)} %copy-done, pred[512,1536]{1,0:T(8,128)(4,1)} %copy-done.7, bf16[3072,4,64]{0,2,1:T(8,128)(2,1)} %get-tuple-element.711, ...), kind=kOutput, calls=%fused_computation.42.clone.1 | convolution fusion | flops 421662208 | bytes 52428808 | tf_op jit(solution)/shard_map/while/body/eval_jaxpr/hqk,khd->qhd/dot_general | solution.py:149
  1058.1 19.3 %fusion.210 = f32[3072,4,64]{0,2,1:T(8,128)} fusion(f32[3072,4,64]{0,2,1:T(8,128)} %get-tuple-element.684, s32[]{:T(128)S(6)} %select_n.270, f32[4,512,1536]{2,1,0:T(8,128)} %fusion.209, f32[4,512,1536]{2,1,0:T(8,128)} %copy-done, pred[512,1536]{1,0:T(8,128)(4,1)} %copy-done.7, bf16[2048,4,64]{0,2,1:T(8,128)(2,1)} %get-tuple-element.708, ...), kind=kOutput, calls=%fused_computation.36.clone.1 | convolution fusion | flops 422317568 | bytes 54525960 | tf_op jit(solution)/shard_map/while/body/eval_jaxpr/hqk,qhd->khd/dot_general | solution.py:153
  1109.8 10.0 fusion.158
  1120.0 11.5 fusion.132
  1141.2 35.2 %reduce-scatter.15.cloned.1.call-done = bf16[512,1024]{1,0:T(8,128)(2,1)} async-done(((bf16[2048,1024]{1,0:T(8,128)(2,1)}), bf16[512,1024]{1,0:T(8,128)(2,1)}) %reduce-scatter.15.cloned.1.call-update) | async-done | bytes 1048592 | tf_op jit(solution)/shard_map/reduce_scatter | solution.py:69
  1191.0 20.4 %all-reduce.4 = (f32[2,256]{1,0:T(2,128)}, f32[1024]{0:T(1024)}) all-reduce(f32[2,256]{1,0:T(2,128)S(1)} %pad_maximum_fusion.3, f32[1024]{0:T(1024)S(1)} %copy-done.51), channel_id=1, replica_groups=mesh['dp'=8,'tensor'=4] {'dp'}, use_global_device_ids=true, to_apply=%region_48.49 | all-reduce | flops 1536 | bytes 12288 | tf_op jit(solution)/shard_map/psum | solution.py:295
  1211.3 15.4 %reduce-scatter.17.cloned.1.call-done = f32[3,128,256]{1,2,0:T(8,128)} async-done(((f32[3,1024,256]{1,2,0:T(8,128)}), f32[3,128,256]{1,2,0:T(8,128)}) %reduce-scatter.17.cloned.1.call-update) | async-done | bytes 393232 | tf_op jit(solution)/shard_map/reduce_scatter | solution.py:290
  1228.7 40.5 %all-reduce.3 = (f32[1024]{0:T(1024)}, f32[1024]{0:T(1024)}, f32[4,1024]{1,0:T(4,128)}, f32[4,1024]{1,0:T(4,128)}) all-reduce(f32[1024]{0:T(1024)S(1)} %copy-done.58, f32[1024]{0:T(1024)S(1)} %copy-done.57, f32[4,1024]{1,0:T(4,128)S(1)} %get-tuple-element.461, ...), channel_id=1, replica_groups=mesh['dp'=8,'tensor'=4] {'dp','tensor'}, use_global_device_ids=true, to_apply=%region_50.51 | all-reduce | flops 10240 | bytes 81920 | tf_op jit(solution)/shard_map/psum | solution.py:298
  1269.2 13.6 reduce-scatter.23.cloned.1.call-done
  1282.8 55.1 %reduce-scatter.21.cloned.1.call-done = f32[128,1024]{1,0:T(8,128)} async-done(((f32[1024,1024]{1,0:T(8,128)}), f32[128,1024]{1,0:T(8,128)}) %reduce-scatter.21.cloned.1.call-update) | async-done | bytes 524304 | tf_op jit(solution)/shard_map/reduce_scatter | solution.py:292
  1338.0 40.2 %reduce-scatter.19.cloned.1.call-done = f32[256,128]{1,0:T(8,128)} async-done(((f32[256,1024]{1,0:T(8,128)}), f32[256,128]{1,0:T(8,128)}) %reduce-scatter.19.cloned.1.call-update) | async-done | bytes 131088 | tf_op jit(solution)/shard_map/reduce_scatter | solution.py:291
  (387 shorter events, 306.2 us)
Async XLA Ops:
  7.2 20.7 %all-to-all-start = ((bf16[8,64,1024]{2,1,0:T(8,128)(2,1)}), bf16[8,64,1024]{2,1,0:T(8,128)(2,1)S(1)}, u32[]{:S(2)}, u32[]{:S(2)}) async-start(bf16[8,64,1024]{2,1,0:T(8,128)(2,1)} %bitcast.172), calls=%async_computation | async-start | bytes 2097152 | tf_op jit(solution)/shard_map/all_to_all | solution.py:179
  12.5 61.0 %all-gather.6.cloned.1.call-start = ((), (), s32[]{:S(2)}) async-start(), calls=%async_computation.12 | async-start | bytes 1769472 | tf_op jit(solution)/shard_map/all_gather | solution.py:193
  32.6 22.2 %collective-permute-start = (bf16[512,1024]{1,0:T(8,128)(2,1)S(1)}, bf16[512,1024]{1,0:T(8,128)(2,1)S(1)}, u32[]{:S(2)}, u32[]{:S(2)}) collective-permute-start(bf16[512,1024]{1,0:T(8,128)(2,1)S(1)} %add_convert_fusion.5), channel_id=1, source_target_pairs={{0,1},{1,0},{2,3},{3,2},{4,5},{5,4},{6,7},{7,6},{8,9},{9,8},{10,11... | collective-permute-start | bytes 3145736 | tf_op jit(solution)/shard_map/ppermute | solution.py:24
  35.1 268.3 %reduce-scatter.9.cloned.1.call-start = ((), (), s32[]{:S(2)}) async-start(), calls=%async_computation.13 | async-start | bytes 5242880 | tf_op jit(solution)/shard_map/reduce_scatter | solution.py:56
  57.2 89.7 %collective-permute-start.1 = (bf16[1024,1024]{1,0:T(8,128)(2,1)}, bf16[1024,1024]{1,0:T(8,128)(2,1)S(1)}, u32[]{:S(2)}, u32[]{:S(2)}) collective-permute-start(bf16[1024,1024]{1,0:T(8,128)(2,1)} %maximum_select_fusion.2), channel_id=1, source_target_pairs={{0,2},{1,3},{2,0},{3,1},{4,6},{5,7},{6,4},{7,5},{8,10},{9,11},{10,... | collective-permute-start | bytes 6291464 | tf_op jit(solution)/shard_map/ppermute | solution.py:24
  221.1 82.4 %copy-start.26 = (f32[1024]{0:T(1024)S(1)}, f32[1024]{0:T(1024)}, u32[]{:S(2)}) copy-start(f32[1024]{0:T(1024)} %param.27) | copy-start | bytes 12292
  221.1 86.2 %copy-start.2 = (bf16[8,64,1024]{2,1,0:T(8,128)(2,1)S(1)}, bf16[8,64,1024]{2,1,0:T(8,128)(2,1)}, u32[]{:S(2)}) copy-start(bf16[8,64,1024]{2,1,0:T(8,128)(2,1)} %copy-done.1) | copy-start | bytes 3145732
  221.1 86.2 %copy-start.35 = (f32[1,1024]{1,0:T(1,128)S(1)}, f32[1,1024]{1,0:T(1,128)}, u32[]{:S(2)}) copy-start(f32[1,1024]{1,0:T(1,128)} %get-tuple-element.445) | copy-start | bytes 12292
  221.1 86.2 %copy-start.54 = (f32[1,1024]{1,0:T(1,128)S(1)}, f32[1,1024]{1,0:T(1,128)}, u32[]{:S(2)}) copy-start(f32[1,1024]{1,0:T(1,128)} %get-tuple-element.449) | copy-start | bytes 12292
  221.1 118.9 %all-gather.8.cloned.1.call-start = ((), (), s32[]{:S(2)}) async-start(), calls=%async_computation.14 | async-start | bytes 2359296 | tf_op jit(solution)/shard_map/all_gather | solution.py:218
  221.9 236.1 %all-gather.10.cloned.1.call-start = ((), (), s32[]{:S(2)}) async-start(), calls=%async_computation.15 | async-start | bytes 2359296 | tf_op jit(solution)/shard_map/all_gather | solution.py:219
  309.6 120.4 %copy-start.60 = (f32[1024]{0:T(1024)S(1)}, f32[1024]{0:T(1024)}, u32[]{:S(2)}) copy-start(f32[1024]{0:T(1024)} %param.28) | copy-start | bytes 12292
  309.6 25.0 %collective-permute-start.2 = (bf16[512,1024]{1,0:T(8,128)(2,1)S(1)}, bf16[512,1024]{1,0:T(8,128)(2,1)S(1)}, u32[]{:S(2)}, u32[]{:S(2)}) collective-permute-start(bf16[512,1024]{1,0:T(8,128)(2,1)S(1)} %add_convert_fusion.2), channel_id=1, source_target_pairs={{0,1},{1,0},{2,3},{3,2},{4,5},{5,4},{6,7},{7,6},{8,9},{9,8},{10,11... | collective-permute-start | bytes 3145736 | tf_op jit(solution)/shard_map/ppermute | solution.py:24
  336.9 93.0 %collective-permute-start.3 = (bf16[1024,1024]{1,0:T(8,128)(2,1)}, bf16[1024,1024]{1,0:T(8,128)(2,1)}, u32[]{:S(2)}, u32[]{:S(2)}) collective-permute-start(bf16[1024,1024]{1,0:T(8,128)(2,1)} %maximum_select_fusion.3), channel_id=1, source_target_pairs={{0,2},{1,3},{2,0},{3,1},{4,6},{5,7},{6,4},{7,5},{8,10},{9,11},{10,... | collective-permute-start | bytes 6291464 | tf_op jit(solution)/shard_map/ppermute | solution.py:24
  339.9 204.5 %reduce-scatter.11.cloned.1.call-start = ((), (), s32[]{:S(2)}) async-start(), calls=%async_computation.16 | async-start | bytes 5242880 | tf_op jit(solution)/shard_map/reduce_scatter | solution.py:56
  467.3 77.1 %copy-start.27 = (f32[1024]{0:T(1024)S(1)}, f32[1024]{0:T(1024)}, u32[]{:S(2)}) copy-start(f32[1024]{0:T(1024)} %param.29) | copy-start | bytes 12292
  467.3 80.9 %all-to-all-start.2 = ((bf16[8,64,1024]{2,1,0:T(8,128)(2,1)}), bf16[8,64,1024]{2,1,0:T(8,128)(2,1)}, u32[]{:S(2)}, u32[]{:S(2)}) async-start(bf16[8,64,1024]{2,1,0:T(8,128)(2,1)} %bitcast.31), calls=%async_computation.4 | async-start | bytes 2097152 | tf_op jit(solution)/shard_map/all_to_all | solution.py:180
  471.6 76.6 %copy-start.37 = (f32[1,1024]{1,0:T(1,128)S(1)}, f32[1,1024]{1,0:T(1,128)}, u32[]{:S(2)}) copy-start(f32[1,1024]{1,0:T(1,128)} %get-tuple-element.447) | copy-start | bytes 12292
  471.6 166.7 %all-gather.12.cloned.1.call-start = ((), (), s32[]{:S(2)}) async-start(), calls=%async_computation.17 | async-start | bytes 5242880 | tf_op jit(solution)/shard_map/all_gather | solution.py:65
  556.9 180.9 %reduce-scatter.13.cloned.1.call-start = ((), (), s32[]{:S(2)}) async-start(), calls=%async_computation.18 | async-start | bytes 5242880 | tf_op jit(solution)/shard_map/reduce_scatter | solution.py:69
  662.3 171.9 %all-gather.14.cloned.1.call-start = ((), (), s32[]{:S(2)}) async-start(), calls=%async_computation.19 | async-start | bytes 5242880 | tf_op jit(solution)/shard_map/all_gather | solution.py:65
  750.1 84.1 %copy-start.25 = (bf16[256,1024]{1,0:T(8,128)(2,1)S(1)}, bf16[256,1024]{1,0:T(8,128)(2,1)}, u32[]{:S(2)}) copy-start(bf16[256,1024]{1,0:T(8,128)(2,1)} %all_gather.23) | copy-start | bytes 1572868
  752.8 423.6 %reduce-scatter.15.cloned.1.call-start = ((), (), s32[]{:S(2)}) async-start(), calls=%async_computation.20 | async-start | bytes 5242880 | tf_op jit(solution)/shard_map/reduce_scatter | solution.py:69
  1100.9 125.8 %reduce-scatter.17.cloned.1.call-start = ((), (), s32[]{:S(2)}) async-start(), calls=%async_computation.21 | async-start | bytes 3538944 | tf_op jit(solution)/shard_map/reduce_scatter | solution.py:290
  1109.8 173.1 %reduce-scatter.23.cloned.1.call-start = ((), (), s32[]{:S(2)}) async-start(), calls=%async_computation.24 | async-start | bytes 4718592 | tf_op jit(solution)/shard_map/reduce_scatter | solution.py:293
  1119.8 218.2 %reduce-scatter.21.cloned.1.call-start = ((), (), s32[]{:S(2)}) async-start(), calls=%async_computation.23 | async-start | bytes 4718592 | tf_op jit(solution)/shard_map/reduce_scatter | solution.py:292
  1132.3 51.6 %all-to-all-start.1 = ((bf16[8,64,1024]{2,1,0:T(8,128)(2,1)}), bf16[8,64,1024]{2,1,0:T(8,128)(2,1)}, u32[]{:S(2)}, u32[]{:S(2)}) async-start(bf16[8,64,1024]{2,1,0:T(8,128)(2,1)} %bitcast.29), calls=%async_computation.3 | async-start | bytes 2097152 | tf_op jit(solution)/shard_map/all_to_all | solution.py:302
  1136.5 39.8 %copy-start.3 = (bf16[8,64,1024]{2,1,0:T(8,128)(2,1)S(1)}, bf16[8,64,1024]{2,1,0:T(8,128)(2,1)}, u32[]{:S(2)}) copy-start(bf16[8,64,1024]{2,1,0:T(8,128)(2,1)} %copy-done.1) | copy-start | bytes 3145732
  1136.5 39.8 %copy-start.30 = (f32[1,1024]{1,0:T(1,128)S(1)}, f32[1,1024]{1,0:T(1,128)}, u32[]{:S(2)}) copy-start(f32[1,1024]{1,0:T(1,128)} %copy-done.29) | copy-start | bytes 12292
  1136.6 39.8 %copy-start.32 = (f32[512]{0:T(512)S(1)}, f32[512]{0:T(512)}, u32[]{:S(2)}) copy-start(f32[512]{0:T(512)} %copy-done.31) | copy-start | bytes 6148
  1136.6 241.6 %reduce-scatter.19.cloned.1.call-start = ((), (), s32[]{:S(2)}) async-start(), calls=%async_computation.22 | async-start | bytes 1179648 | tf_op jit(solution)/shard_map/reduce_scatter | solution.py:291
  1183.9 85.3 %all-to-all-start.3 = ((bf16[8,64,1024]{2,1,0:T(8,128)(2,1)}), bf16[8,64,1024]{2,1,0:T(8,128)(2,1)}, u32[]{:S(2)}, u32[]{:S(2)}) async-start(bf16[8,64,1024]{2,1,0:T(8,128)(2,1)} %bitcast.167), calls=%async_computation.7 | async-start | bytes 2097152 | tf_op jit(solution)/shard_map/all_to_all | solution.py:303
  (67 other events, 714.5 us)
Sparse Core Ops, SparseCore 0:
  35.2 24.2 all-gather.5
  221.2 82.1 reduce-scatter.8
  305.5 28.3 all-gather.7
  340.0 26.6 all-gather.9
  467.4 76.8 reduce-scatter.10
  557.0 81.2 all-gather.11
  662.4 75.2 reduce-scatter.12
  752.9 81.2 all-gather.13
  1101.0 75.2 reduce-scatter.14
  1179.6 47.0 reduce-scatter.16
  1231.0 51.7 reduce-scatter.22
  1286.6 51.3 reduce-scatter.20
  1342.0 36.0 reduce-scatter.18
